TPU v7x, 32 devices: a whole 2x2x4 slice. The times are simulated.
32 devices in a mesh: dp: 4 (over y, x), tp: 8 (over z, core).
Axes of the slice: x: 2, y: 2, z: 4, core: 2. Of those that a mesh axis runs over, the one named last changes fastest.
Arguments:
- hidden_in: bfloat16 [4, 32, 4096], P(None, 'dp'), may hold values from -6 to 6
- pre_gain: float32 [4096], replicated, may hold values from 0.25 to 1.75
- w_zx: bfloat16 [4096, 2, 8192], P(None, None, 'tp'), may hold values from -0.09375 to 0.09375
- zx_codes: bfloat16 [4096, 2, 8192], P(('dp', 'tp')), may hold values from -4 to 4
- zx_exponents: int32 [32, 2, 64], P('dp', None, 'tp'), may hold values from -9 to -6
- w_bc: bfloat16 [4096, 2048], P(None, 'tp'), may hold values from -0.09375 to 0.09375
- w_dt: bfloat16 [4096, 128], P(None, 'tp'), may hold values from -0.09375 to 0.09375
- conv_x: float32 [5, 8192], P(None, 'tp'), may hold values from -0.6 to 0.6
- conv_bc: float32 [5, 2048], P(None, 'tp'), may hold values from -0.6 to 0.6
- dt_bias: float32 [128], P('tp'), may hold values from -2 to 0.5
- decay_rate: float32 [128], P('tp'), may hold values from 0.05 to 2
- skip_gain: float32 [128], P('tp'), may hold values from 0.5 to 1.5
- conv_state_x: bfloat16 [32, 3, 8192], P('dp', None, 'tp'), may hold values from -6 to 6
- conv_state_bc: bfloat16 [32, 3, 2048], P('dp', None, 'tp'), may hold values from -6 to 6
- ssm_state: float32 [32, 128, 64, 256], P('dp', 'tp'), may hold values from -6 to 6
- norm_gain: float32 [8192], P('tp'), may hold values from 0.25 to 1.75
- w_out: bfloat16 [8192, 4096], P('tp'), may hold values from -0.0625 to 0.0625
- out_codes: bfloat16 [8192, 4096], P('tp', 'dp'), may hold values from -4 to 4
- out_exponents: int32 [64, 32], P('tp', 'dp'), may hold values from -7 to -4
Outputs:
- mixed: bfloat16 [4, 32, 4096], P(None, 'dp', 'tp')
- final_state: float32 [32, 128, 64, 256], P('dp', 'tp')
All inputs are finite; a program needn't handle non-finite values.
Results may differ from a plain program's by a relative error of at most 0.014.
Values may be sent and summed in bfloat16 or wider, within the bound.
A program may use at most 192 MiB of HBM per device.

v0:
```python
import jax
import jax.numpy as jnp
from jax import lax
from jax.sharding import PartitionSpec as P

D = 4096
H = 128
G = 4
BLK = 128
STEPS = 4
DI = 8192


EPS = 1e-05


def decode_pairs(codes, exponents, block):
    rows, pair, cols = codes.shape
    blocked = codes.astype(jnp.float32).reshape(rows // block, block, pair, cols // block, block)
    scales = jnp.exp2(exponents.astype(jnp.float32))
    return (blocked * scales[:, None, :, :, None]).reshape(rows, pair, cols)


def decode_matrix(codes, exponents, block):
    rows, cols = codes.shape
    blocked = codes.astype(jnp.float32).reshape(rows // block, block, cols // block, block)
    scales = jnp.exp2(exponents.astype(jnp.float32))
    return (blocked * scales[:, None, :, None]).reshape(rows, cols)


def conv_step(history, fresh, params):
    window = jnp.concatenate([history, fresh[:, None, :]], axis=1)
    mixed = jnp.sum(window * params[:4][None], axis=1) + params[4]
    return (jax.nn.silu(mixed), window[:, 1:])


def body(
    hidden_in,
    pre_gain,
    w_zx,
    zx_codes,
    zx_exponents,
    w_bc,
    w_dt,
    conv_x,
    conv_bc,
    dt_bias,
    decay_rate,
    skip_gain,
    conv_state_x,
    conv_state_bc,
    ssm_state,
    norm_gain,
    w_out,
    out_codes,
    out_exponents,
):
    slot = lax.axis_index("tp")
    tp_count = lax.axis_size("tp")
    traded = lax.all_to_all(zx_codes, "tp", split_axis=2, concat_axis=0, tiled=True)
    zx_delta = decode_pairs(traded, zx_exponents, BLK)
    local_cols = traded.shape[2]
    gathered = lax.all_gather(zx_delta.astype(jnp.bfloat16), "dp", axis=0, tiled=True)
    zx_weights = (
        (w_zx.astype(jnp.float32) + gathered.astype(jnp.float32))
        .astype(jnp.bfloat16)
        .reshape(D, 2 * local_cols)
    )
    out_piece = decode_matrix(out_codes, out_exponents, BLK).astype(jnp.bfloat16)
    out_full = lax.all_gather(out_piece, "dp", axis=1, tiled=True)
    new_out = (w_out.astype(jnp.float32) + out_full.astype(jnp.float32)).astype(jnp.bfloat16)
    heads_here = ssm_state.shape[1]
    states_n = ssm_state.shape[3]
    group = slot * heads_here // (H // G)
    group_mask = (jnp.arange(G) == group).astype(jnp.float32)
    history_x = conv_state_x.astype(jnp.float32)
    history_bc = conv_state_bc.astype(jnp.float32)
    state = ssm_state
    results = []
    carried = None
    for step in range(STEPS):
        x = hidden_in[step].astype(jnp.float32)
        if step > 0:
            x = x + carried.astype(jnp.float32)
        rows = x.shape[0]
        normed = (x * lax.rsqrt(jnp.mean(x * x, -1, keepdims=True) + EPS) * pre_gain).astype(
            jnp.bfloat16
        )
        zx = jnp.dot(normed, zx_weights, preferred_element_type=jnp.float32)
        zx = zx.reshape(rows, 2, local_cols)
        gate = zx[:, 0]
        inner = zx[:, 1]
        bc_raw = jnp.dot(normed, w_bc, preferred_element_type=jnp.float32)
        dt_raw = jnp.dot(normed, w_dt, preferred_element_type=jnp.float32)
        conv_inner, history_x = conv_step(history_x, inner, conv_x)
        conv_piece, history_bc = conv_step(history_bc, bc_raw, conv_bc)
        bc_all = lax.all_gather(conv_piece, "tp", axis=1, tiled=True)
        b_group = lax.dynamic_slice_in_dim(bc_all, group * states_n, states_n, 1)
        c_group = lax.dynamic_slice_in_dim(bc_all, G * states_n + group * states_n, states_n, 1)
        step_size = jax.nn.softplus(dt_raw + dt_bias)
        decay = jnp.exp(-step_size * decay_rate)
        inner_heads = conv_inner.reshape(rows, heads_here, -1)
        state = (
            decay[:, :, None, None] * state
            + (step_size[:, :, None] * inner_heads)[:, :, :, None] * b_group[:, None, None, :]
        )
        read = (
            jnp.einsum("rhpn,rn->rhp", state, c_group, precision=lax.Precision.HIGHEST)
            + skip_gain[:, None] * inner_heads
        )
        gated = read.reshape(rows, local_cols) * jax.nn.silu(gate)
        squares = jnp.sum(gated * gated, -1)
        totals = lax.psum(squares[:, None] * group_mask, "tp")
        mean_sq = jnp.sum(totals * group_mask, -1) / (DI // G)
        scaled = (gated * lax.rsqrt(mean_sq + EPS)[:, None] * norm_gain).astype(jnp.bfloat16)
        partial_value = jnp.dot(scaled, new_out, preferred_element_type=jnp.float32)
        whole = lax.psum(partial_value, "tp").astype(jnp.bfloat16)
        width = partial_value.shape[1] // tp_count
        results.append(lax.dynamic_slice_in_dim(whole, slot * width, width, 1))
        carried = whole
    return (jnp.stack(results), state)


def solution(mesh):
    return jax.shard_map(
        body,
        mesh=mesh,
        in_specs=(
            P(None, "dp", None),
            P(),
            P(None, None, "tp"),
            P(("dp", "tp"), None, None),
            P("dp", None, "tp"),
            P(None, "tp"),
            P(None, "tp"),
            P(None, "tp"),
            P(None, "tp"),
            P("tp"),
            P("tp"),
            P("tp"),
            P("dp", None, "tp"),
            P("dp", None, "tp"),
            P("dp", "tp", None, None),
            P("tp"),
            P("tp", None),
            P("tp", "dp"),
            P("tp", "dp"),
        ),
        out_specs=(P(None, "dp", "tp"), P("dp", "tp", None, None)),
        check_vma=False,
    )
```

profile of v0, /device:TPU:0, one launch (start us, length us, event | category | flops | bytes accessed | tf_op | source)
XLA Modules:
  0.0 712.7 jit_solution(7525767807919478908)
XLA Ops:
  7.2 0.8 multiply_exponential_fusion.4
  8.1 0.3 mul.639
  8.4 4.1 fusion.3
  12.6 15.0 %copy.29 = bf16[128,2,8192]{0,1,2:T(2,128)(2,1)} copy(bf16[128,2,8192]{2,1,0:T(2,128)(2,1)} %param.22) | data formatting | bytes 8388608 | tf_op args[3]
  27.6 6.4 all-to-all-start
  34.1 4.0 mul.609
  38.1 10.8 %mul.610 = f32[1024,2,1024]{2,1,0:T(2,128)} reshape(f32[8,128,2,8,128]{4,3,2,1,0:T(8,128)} %mul.609) | data formatting | bytes 16777216 | tf_op jit(solution)/shard_map/mul | solution.py:21
  48.8 79.2 %all-to-all-done = bf16[128,2,8192]{0,1,2:T(2,128)(2,1)} async-done(((bf16[128,2,8192]{0,1,2:T(2,128)(2,1)}), bf16[128,2,8192]{0,1,2:T(2,128)(2,1)}, u32[]{:S(2)}, u32[]{:S(2)}) %all-to-all-start) | async-done | bytes 4194336 | tf_op jit(solution)/shard_map/all_to_all | solution.py:60
  128.1 8.5 %convert_bitcast_fusion = f32[8,128,2,1024]{1,2,3,0:T(2,128)} fusion(bf16[128,2,8,1024]{0,1,3,2:T(2,128)(2,1)} %bitcast.39), kind=kLoop, calls=%fused_computation.2 | loop fusion | flops 2097152 | bytes 12582912 | tf_op jit(solution)/shard_map/convert_element_type | solution.py:19
  136.5 17.1 %copy.30 = f32[8,128,2,1024]{3,2,1,0:T(2,128)} copy(f32[8,128,2,1024]{1,2,3,0:T(2,128)} %convert_bitcast_fusion) | data formatting | bytes 16777216 | tf_op jit(solution)/shard_map/convert_element_type | solution.py:19
  153.7 9.0 %fusion = bf16[1024,2,1024]{2,1,0:T(2,128)(2,1)} fusion(f32[1024,2,1024]{2,1,0:T(2,128)} %mul.610, f32[8,128,2,1024]{3,2,1,0:T(2,128)} %copy.30), kind=kLoop, calls=%fused_computation.4 | loop fusion | flops 4194304 | bytes 20971520 | tf_op jit(solution)/shard_map/convert_element_type | solution.py:63
  163.2 0.4 convolution_bitcast_fusion.3
  163.6 14.2 %all_gather.19 = f32[8,2048]{1,0:T(8,128)S(1)} all-gather(f32[8,256]{1,0:T(8,128)S(1)} %divide_multiply_fusion.7), channel_id=1, replica_groups=mesh['dp'=4,'tp'=8] {'tp'}, dimensions={1}, use_global_device_ids=true | all-gather | bytes 73728 | tf_op jit(solution)/shard_map/all_gather | solution.py:97
  178.1 10.1 %add_convert_fusion.1 = bf16[1024,4096]{1,0:T(8,128)(2,1)} fusion(bf16[1024,4096]{1,0:T(8,128)(2,1)} %all-gather.5.cloned.1.call-done, bf16[1024,4096]{1,0:T(8,128)(2,1)} %param.35), kind=kLoop, calls=%fused_computation.1 | loop fusion | flops 16777216 | bytes 25165824 | tf_op jit(solution)/shard_map/convert_element_type | solution.py:71
  188.2 131.0 %all-gather.3.cloned.1.call-done = bf16[4096,2,1024]{2,1,0:T(2,128)(2,1)} async-done(((bf16[1024,2,1024]{2,1,0:T(2,128)(2,1)}), bf16[4096,2,1024]{2,1,0:T(2,128)(2,1)}) %all-gather.3.cloned.1.call-update) | async-done | bytes 16777232 | tf_op jit(solution)/shard_map/all_gather | solution.py:63
  319.1 19.2 %add_convert_fusion = bf16[4096,2,1024]{2,1,0:T(2,128)(2,1)S(1)} fusion(bf16[4096,2,1024]{2,1,0:T(2,128)(2,1)} %all-gather.3.cloned.1.call-done, bf16[4096,2,1024]{2,1,0:T(2,128)(2,1)} %param.21), kind=kLoop, calls=%fused_computation | loop fusion | flops 33554432 | bytes 50331648 | tf_op jit(solution)/shard_map/convert_element_type | solution.py:66
  338.3 9.3 %copy.40 = bf16[512,8,2,1024]{3,1,2,0:T(8,128)(2,1)} copy(bf16[512,8,2,1024]{3,2,1,0:T(2,128)(2,1)S(1)} %bitcast.210) | data formatting | bytes 33554432
  347.6 20.7 %copy.31 = bf16[2048,4096]{1,0:T(8,128)(2,1)} copy(bf16[2048,4096]{0,1:T(8,128)(2,1)} %bitcast.211) | data formatting | bytes 33554432 | tf_op jit(solution)/shard_map/dot_general | solution.py:89
  368.3 10.2 %fusion.29 = f32[8,2,1024]{2,0,1:T(8,128)S(1)} fusion(bf16[2,1024,4096]{2,1,0:T(8,128)(2,1)} %bitcast.206, f32[4096]{0:T(1024)S(1)} %copy-done.5, f32[8]{0:T(128)S(1)} %add_rsqrt_fusion.7, bf16[4,8,4096]{2,1,0:T(8,128)(2,1)S(1)} %copy-done.2), kind=kOutput, calls=%fused_computation.67 | convolution fusion | flops 134348800 | bytes 16925184 | tf_op jit(solution)/shard_map/dot_general | solution.py:89
  378.8 13.1 %fusion.1 = f32[8,1,16,64]{3,1,2,0:T(1,128)S(1)} fusion(f32[8,16,64,256]{3,2,1,0:T(8,128)} %param.33, f32[8,256]{1,0:T(8,128)S(1)} %get-tuple-element.23, f32[8,16,64]{2,1,0:T(8,128)S(1)} %broadcast_multiply_fusion.3, f32[8,16]{1,0:T(8,128)S(1)} %get-tuple-element.26, f32[8,256,1,1]{1,0,2,3:T(8,128)S(1)} %get-tuple-element.22), kind=kOutput, calls=%fused_computation.9 | convolution fusion | flops 31457280 | bytes 8471040 | tf_op jit(solution)/shard_map/rhpn,rn->rhp/dot_general | solution.py:108
  391.9 0.2 multiply_reduce_fusion.6
  392.2 16.4 %psum.56 = f32[8,4]{0,1:T(4,128)S(1)} all-reduce(f32[8,4]{0,1:T(4,128)S(1)} %broadcast_multiply_fusion.7), channel_id=1, replica_groups=mesh['dp'=4,'tp'=8] {'tp'}, use_global_device_ids=true, to_apply=%region_4.5 | all-reduce | flops 32 | bytes 256 | tf_op jit(solution)/shard_map/psum | solution.py:113
  408.8 4.6 fusion.84
  413.4 27.1 %all-reduce.4 = bf16[8,4096]{1,0:T(8,128)(2,1)S(1)} all-reduce(f32[8,4096]{1,0:T(8,128)S(1)} %fusion.84), channel_id=1, replica_groups=mesh['dp'=4,'tp'=8] {'tp'}, use_global_device_ids=true, to_apply=%region_6.7 | all-reduce | flops 32768 | bytes 196608 | tf_op jit(solution)/shard_map/psum | solution.py:117
  440.8 10.2 %fusion.35 = f32[8,2,1024]{2,0,1:T(8,128)S(1)} fusion(bf16[2,1024,4096]{2,1,0:T(8,128)(2,1)} %bitcast.207, bf16[8,4096]{1,0:T(8,128)(2,1)S(1)} %multiply_convert_fusion.2), kind=kOutput, calls=%fused_computation.72 | convolution fusion | flops 134217728 | bytes 16908288 | tf_op jit(solution)/shard_map/dot_general | solution.py:89
  451.2 0.4 convolution_bitcast_fusion.2
  451.7 14.0 %all_gather.21 = f32[8,2048]{1,0:T(8,128)S(1)} all-gather(f32[8,256]{1,0:T(8,128)S(1)} %divide_multiply_fusion.6), channel_id=1, replica_groups=mesh['dp'=4,'tp'=8] {'tp'}, dimensions={1}, use_global_device_ids=true | all-gather | bytes 73728 | tf_op jit(solution)/shard_map/all_gather | solution.py:97
  465.9 13.7 %fusion.10 = f32[8,1,16,64]{3,1,2,0:T(1,128)S(1)} fusion(f32[8,16,64,256]{3,2,1,0:T(8,128)} %param.33, f32[8,256]{1,0:T(8,128)S(1)} %get-tuple-element.19, f32[8,16,64]{2,1,0:T(8,128)S(1)} %broadcast_multiply_fusion.2, f32[8,16]{1,0:T(8,128)S(1)} %get-tuple-element.28, f32[8,256]{1,0:T(8,128)S(1)} %get-tuple-element.23, ...), kind=kOutput, calls=%fused_computation.19 | convolution fusion | flops 37748736 | bytes 8512512 | tf_op jit(solution)/shard_map/rhpn,rn->rhp/dot_general | solution.py:108
  479.9 13.9 %psum.58 = f32[8,4]{0,1:T(4,128)S(1)} all-reduce(f32[8,4]{0,1:T(4,128)S(1)} %broadcast_multiply_fusion.6), channel_id=1, replica_groups=mesh['dp'=4,'tp'=8] {'tp'}, use_global_device_ids=true, to_apply=%region_11.12 | all-reduce | flops 32 | bytes 256 | tf_op jit(solution)/shard_map/psum | solution.py:113
  493.9 4.6 fusion.82
  498.6 27.7 %all-reduce.5 = bf16[8,4096]{1,0:T(8,128)(2,1)S(1)} all-reduce(f32[8,4096]{1,0:T(8,128)S(1)} %fusion.82), channel_id=1, replica_groups=mesh['dp'=4,'tp'=8] {'tp'}, use_global_device_ids=true, to_apply=%region_13.14 | all-reduce | flops 32768 | bytes 196608 | tf_op jit(solution)/shard_map/psum | solution.py:117
  526.5 10.2 %fusion.33 = f32[8,2,1024]{2,0,1:T(8,128)S(1)} fusion(bf16[2,1024,4096]{2,1,0:T(8,128)(2,1)} %bitcast.208, bf16[8,4096]{1,0:T(8,128)(2,1)S(1)} %multiply_convert_fusion.1), kind=kOutput, calls=%fused_computation.70 | convolution fusion | flops 134217728 | bytes 16908288 | tf_op jit(solution)/shard_map/dot_general | solution.py:89
  536.9 0.4 convolution_bitcast_fusion.1
  537.4 14.0 %all_gather.22 = f32[8,2048]{1,0:T(8,128)S(1)} all-gather(f32[8,256]{1,0:T(8,128)S(1)} %divide_multiply_fusion.5), channel_id=1, replica_groups=mesh['dp'=4,'tp'=8] {'tp'}, dimensions={1}, use_global_device_ids=true | all-gather | bytes 73728 | tf_op jit(solution)/shard_map/all_gather | solution.py:97
  551.6 14.5 %fusion.2 = f32[8,1,16,64]{3,1,2,0:T(1,128)S(1)} fusion(f32[8,256]{1,0:T(8,128)S(1)} %get-tuple-element.15, f32[8,16,64]{2,1,0:T(8,128)S(1)} %broadcast_multiply_fusion.1, f32[8,16]{1,0:T(8,128)S(1)} %get-tuple-element.30, f32[8,16,64,256]{3,2,1,0:T(8,128)} %param.33, f32[8,256]{1,0:T(8,128)S(1)} %get-tuple-element.19, ...), kind=kOutput, calls=%fused_computation.10 | convolution fusion | flops 44040192 | bytes 8553984 | tf_op jit(solution)/shard_map/rhpn,rn->rhp/dot_general | solution.py:108
  566.4 13.9 %psum.60 = f32[8,4]{0,1:T(4,128)S(1)} all-reduce(f32[8,4]{0,1:T(4,128)S(1)} %broadcast_multiply_fusion.5), channel_id=1, replica_groups=mesh['dp'=4,'tp'=8] {'tp'}, use_global_device_ids=true, to_apply=%region_18.19 | all-reduce | flops 32 | bytes 256 | tf_op jit(solution)/shard_map/psum | solution.py:113
  580.5 4.6 fusion.80
  585.1 27.2 %all-reduce.6 = bf16[8,4096]{1,0:T(8,128)(2,1)S(1)} all-reduce(f32[8,4096]{1,0:T(8,128)S(1)} %fusion.80), channel_id=1, replica_groups=mesh['dp'=4,'tp'=8] {'tp'}, use_global_device_ids=true, to_apply=%region_20.21 | all-reduce | flops 32768 | bytes 196608 | tf_op jit(solution)/shard_map/psum | solution.py:117
  612.6 10.2 %fusion.31 = f32[8,2,1024]{2,0,1:T(8,128)S(1)} fusion(bf16[2,1024,4096]{2,1,0:T(8,128)(2,1)} %bitcast.209, bf16[8,4096]{1,0:T(8,128)(2,1)S(1)} %multiply_convert_fusion), kind=kOutput, calls=%fused_computation.68 | convolution fusion | flops 134217728 | bytes 16908288 | tf_op jit(solution)/shard_map/dot_general | solution.py:89
  623.0 0.4 convolution_bitcast_fusion
  623.5 14.2 %all_gather.23 = f32[8,2048]{1,0:T(8,128)S(1)} all-gather(f32[8,256]{1,0:T(8,128)S(1)} %divide_multiply_fusion.4), channel_id=1, replica_groups=mesh['dp'=4,'tp'=8] {'tp'}, dimensions={1}, use_global_device_ids=true | all-gather | bytes 73728 | tf_op jit(solution)/shard_map/all_gather | solution.py:97
  637.8 7.7 %multiply_add_fusion = f32[8,16,64,256]{3,2,1,0:T(8,128)S(1)} fusion(f32[8,256]{1,0:T(8,128)S(1)} %get-tuple-element.11, f32[8,16,64]{2,1,0:T(8,128)S(1)} %broadcast_multiply_fusion, f32[8,16]{1,0:T(8,128)S(1)} %get-tuple-element.32, f32[8,256]{1,0:T(8,128)S(1)} %get-tuple-element.15, f32[8,16,64]{2,1,0:T(8,128)S(1)} %broadcast_multiply_fusion.1, ...), kind=kLoop, calls=%fused_computation.5 | loop fusion | flops 25165824 | bytes 16943104 | tf_op jit(solution)/shard_map/add | solution.py:104
  645.5 3.4 copy-done.1
  648.9 9.8 %fusion.99 = f32[8,1,16,64]{3,1,2,0:T(1,128)S(1)} fusion(f32[8,16,64,256]{3,2,1,0:T(8,128)S(1)} %multiply_add_fusion, f32[8,256,1,1]{1,0,2,3:T(8,128)S(1)} %get-tuple-element.10), kind=kOutput, calls=%fused_computation.172 | convolution fusion | flops 25165824 | bytes 8429568 | tf_op jit(solution)/shard_map/rhpn,rn->rhp/dot_general | solution.py:108
  659.1 13.9 %psum.62 = f32[8,4]{0,1:T(4,128)S(1)} all-reduce(f32[8,4]{0,1:T(4,128)S(1)} %broadcast_multiply_fusion.4), channel_id=1, replica_groups=mesh['dp'=4,'tp'=8] {'tp'}, use_global_device_ids=true, to_apply=%region_25.26 | all-reduce | flops 32 | bytes 256 | tf_op jit(solution)/shard_map/psum | solution.py:113
  673.2 4.6 fusion.78
  677.8 27.2 %all-reduce.7 = bf16[8,4096]{1,0:T(8,128)(2,1)S(1)} all-reduce(f32[8,4096]{1,0:T(8,128)S(1)} %fusion.78), channel_id=1, replica_groups=mesh['dp'=4,'tp'=8] {'tp'}, use_global_device_ids=true, to_apply=%region_27.28 | all-reduce | flops 32768 | bytes 196608 | tf_op jit(solution)/shard_map/psum | solution.py:117
  705.0 0.6 pad_maximum_fusion.6
  (117 shorter events, 4.9 us)
Async XLA Ops:
  7.2 156.0 %copy-start = (bf16[4096,256]{1,0:T(8,128)(2,1)S(1)}, bf16[4096,256]{1,0:T(8,128)(2,1)}, u32[]{:S(2)}) copy-start(bf16[4096,256]{1,0:T(8,128)(2,1)} %param.24) | copy-start | bytes 6291460
  7.2 170.9 %all-gather.5.cloned.1.call-start = ((), (), s32[]{:S(2)}) async-start(), calls=%async_computation.2 | async-start | bytes 10485760 | tf_op jit(solution)/shard_map/all_gather | solution.py:70
  12.6 21.5 %copy-start.10 = (s32[8,2,8]{2,1,0:T(2,128)S(1)}, s32[8,2,8]{2,1,0:T(2,128)}, u32[]{:S(2)}) copy-start(s32[8,2,8]{2,1,0:T(2,128)} %param.23) | copy-start | bytes 1540
  27.6 100.5 %all-to-all-start = ((bf16[128,2,8192]{0,1,2:T(2,128)(2,1)}), bf16[128,2,8192]{0,1,2:T(2,128)(2,1)}, u32[]{:S(2)}, u32[]{:S(2)}) async-start(bf16[128,2,8192]{0,1,2:T(2,128)(2,1)} %copy.29), calls=%async_computation | async-start | bytes 8388608 | tf_op jit(solution)/shard_map/all_to_all | solution.py:60
  34.0 285.2 %all-gather.3.cloned.1.call-start = ((), (), s32[]{:S(2)}) async-start(), calls=%async_computation.1 | async-start | bytes 20971520 | tf_op jit(solution)/shard_map/all_gather | solution.py:63
  153.6 9.1 %copy-start.13 = (f32[5,256]{1,0:T(8,128)S(1)}, f32[5,256]{1,0:T(8,128)}, u32[]{:S(2)}) copy-start(f32[5,256]{1,0:T(8,128)} %param.27) | copy-start | bytes 15364
  153.6 9.2 %copy-start.8 = (bf16[8,3,256]{2,0,1:T(8,128)(2,1)S(1)}, bf16[8,3,256]{2,0,1:T(8,128)(2,1)}, u32[]{:S(2)}) copy-start(bf16[8,3,256]{2,0,1:T(8,128)(2,1)} %param.32) | copy-start | bytes 36868
  153.6 9.2 %copy-start.7 = (f32[5,1024]{1,0:T(8,128)S(1)}, f32[5,1024]{1,0:T(8,128)}, u32[]{:S(2)}) copy-start(f32[5,1024]{1,0:T(8,128)} %param.26) | copy-start | bytes 61444
  153.6 9.2 %copy-start.6 = (bf16[8,3,1024]{2,0,1:T(8,128)(2,1)S(1)}, bf16[8,3,1024]{2,0,1:T(8,128)(2,1)}, u32[]{:S(2)}) copy-start(bf16[8,3,1024]{2,0,1:T(8,128)(2,1)} %param.31) | copy-start | bytes 147460
  153.6 9.3 %copy-start.2 = (bf16[4,8,4096]{2,1,0:T(8,128)(2,1)S(1)}, bf16[4,8,4096]{2,1,0:T(8,128)(2,1)}, u32[]{:S(2)}) copy-start(bf16[4,8,4096]{2,1,0:T(8,128)(2,1)} %param.19) | copy-start | bytes 786436
  153.6 9.5 %copy-start.5 = (f32[4096]{0:T(1024)S(1)}, f32[4096]{0:T(1024)}, u32[]{:S(2)}) copy-start(f32[4096]{0:T(1024)} %param.20) | copy-start | bytes 49156
  153.7 24.1 %copy-start.3 = (bf16[4096,16]{0,1:T(8,128)(2,1)S(1)}, bf16[4096,16]{0,1:T(8,128)(2,1)}, u32[]{:S(2)}) copy-start(bf16[4096,16]{0,1:T(8,128)(2,1)} %param.25) | copy-start | bytes 393220
  153.7 24.1 %copy-start.11 = (f32[16]{0:T(128)S(1)}, f32[16]{0:T(128)}, u32[]{:S(2)}) copy-start(f32[16]{0:T(128)} %param.29) | copy-start | bytes 196
  153.7 24.1 %copy-start.12 = (f32[16]{0:T(128)S(1)}, f32[16]{0:T(128)}, u32[]{:S(2)}) copy-start(f32[16]{0:T(128)} %param.28) | copy-start | bytes 196
  378.5 13.4 %copy-start.9 = (f32[16]{0:T(128)S(1)}, f32[16]{0:T(128)}, u32[]{:S(2)}) copy-start(f32[16]{0:T(128)} %param.30) | copy-start | bytes 196
  378.5 30.2 %copy-start.4 = (f32[1024]{0:T(1024)S(1)}, f32[1024]{0:T(1024)}, u32[]{:S(2)}) copy-start(f32[1024]{0:T(1024)} %param.34) | copy-start | bytes 12292
  645.5 3.4 copy-start.1
Sparse Core Ops, SparseCore 0:
  12.7 90.1 all-gather.4
  162.9 156.2 all-gather.2
where the time goes:
time: 721 us; the launch traced here: 713 us
  blocking collectives  224 us (31%)
  waiting for transfers between devices  210 us (29%)
  matrix products  113 us (16%)
  local copies, waits for them, and re-layouts  81.8 us (11%)
  other arithmetic  63.1 us (9%)
  between operations  14.8 us (2%)
    all_gather x1, waiting for transfers between devices, body(): lax.all_gather(zx_delta.astype(jnp.bfloat16), 'dp', axis=0, tiled=True)  131 us
    psum x4, blocking collectives, body(): whole = lax.psum(partial_value, 'tp').astype(jnp.bfloat16)  109 us
    all_to_all x1, waiting for transfers between devices, body(): lax.all_to_all(zx_codes, 'tp', split_axis=2, concat_axis=0, tiled=True)  79.2 us
    psum x4, blocking collectives, body(): totals = lax.psum(squares[:, None] * group_mask, 'tp')  58.1 us
    all_gather x4, blocking collectives, body(): bc_all = lax.all_gather(conv_piece, 'tp', axis=1, tiled=True)  56.3 us
    dot_general x4, matrix products, body(): jnp.einsum('rhpn,rn->rhp', state, c_group, precision=lax.Precision.HIGHEST)  51.1 us
    dot_general x4, matrix products, body(): zx = jnp.dot(normed, zx_weights, preferred_element_type=jnp.float32)  40.7 us
    unnamed x30, local copies, waits for them, and re-layouts  27.7 us
  transfers between devices with their start and end apart: 3, of which 2 were waited for; matrix products, arithmetic and copies ran while one was open for 11% of the time, Pallas kernels for 0%

commit v1 on v0

v1 whole, which is shorter than its diff:
```python
import jax
import jax.numpy as jnp
from jax import lax
from jax.experimental import pallas as pl
from jax.experimental.pallas import tpu as pltpu
from jax.sharding import PartitionSpec as P

G = 4
BLK = 128
LANES = 128
EPS = 1e-05
MESH = pl.DeviceIdType.MESH
F32 = jnp.float32
BF16 = jnp.bfloat16


def decode_pairs(codes, exponents, block):
    rows, pair, cols = codes.shape
    blocked = codes.astype(F32).reshape(rows // block, block, pair, cols // block, block)
    scales = jnp.exp2(exponents.astype(F32))
    return (blocked * scales[:, None, :, :, None]).reshape(rows, pair, cols)


def decode_matrix(codes, exponents, block):
    rows, cols = codes.shape
    blocked = codes.astype(F32).reshape(rows // block, block, cols // block, block)
    scales = jnp.exp2(exponents.astype(F32))
    return (blocked * scales[:, None, :, None]).reshape(rows, cols)


def silu(v):
    return v / (1.0 + jnp.exp(-v))


def make_kernel(ndp, ntp, steps, rows, dc, lc, cb, heads, psize, nstate, gsz, feats, di):
    oc = feats // ntp
    ac = dc // ntp
    nchunk = lc // LANES
    hpc = LANES // psize
    small = cb + LANES

    def kernel(
        hid_ref, gain_ref, wz_ref, ws_ref, wo_ref, convx_ref, convb_ref, dtb_ref, rate_ref,
        skip_ref, ng_ref, hx0_ref, hb0_ref, state_hbm,
        out_ref, state_out,
        state, hx, hb, hrecv, s1, r1, s2, r2, cs, cr, gs, gr, qs, qr, os, orv, ags, agr, ms, mr,
        tbuf, rbuf,
        st_sem, send_sem, h_sem, sem1, sem2, c_sem, g_sem, q_sem, o_sem, a_sem, m_sem,
    ):
        dp = lax.axis_index("dp")
        tp = lax.axis_index("tp")
        pending = []

        def send(src, dst, rsem, d, t):
            copy = pltpu.make_async_remote_copy(
                src_ref=src, dst_ref=dst, send_sem=send_sem, recv_sem=rsem,
                device_id=(d, t), device_id_type=MESH,
            )
            copy.start()
            pending.append(copy)

        def recv(src, dst, rsem):
            pltpu.make_async_remote_copy(
                src_ref=src, dst_ref=dst, send_sem=send_sem, recv_sem=rsem,
                device_id=(dp, tp), device_id_type=MESH,
            ).wait_recv()

        load = pltpu.make_async_copy(state_hbm, state, st_sem)
        load.start()

        barrier = pltpu.get_barrier_semaphore()
        for i in range(ndp):
            for j in range(ntp):
                if i + j > 0:
                    pl.semaphore_signal(
                        barrier, inc=1,
                        device_id=(lax.rem(dp + i, ndp), lax.rem(tp + j, ntp)),
                        device_id_type=MESH,
                    )
        pl.semaphore_wait(barrier, ndp * ntp - 1)

        for k in range(1, ndp):
            peer = lax.rem(dp + k, ndp)
            send(hid_ref.at[peer], hrecv.at[dp], h_sem.at[k], peer, tp)
        hrecv[dp] = hid_ref[dp]
        hx[0:3] = hx0_ref[...].astype(F32)
        hb[0:3] = hb0_ref[...].astype(F32)
        for k in range(1, ndp):
            src = lax.rem(dp + ndp - k, ndp)
            recv(hid_ref.at[src], hrecv.at[src], h_sem.at[k])

        lane = lax.broadcasted_iota(jnp.int32, (rows, LANES), 1)
        lane_all = lax.broadcasted_iota(jnp.int32, (ndp * rows, LANES), 1)
        lane_sq = lax.broadcasted_iota(jnp.int32, (LANES, LANES), 1)
        owner = tp * oc // dc
        half = (tp * oc - owner * dc) // oc
        group = tp // gsz
        member = tp - group * gsz
        carried = None
        for s in range(steps):
            x = jnp.concatenate([hrecv[d, s].astype(F32) for d in range(ndp)], axis=0)
            if s > 0:
                x = x + carried
            ss = jnp.sum(x * x, axis=1, keepdims=True)
            y = (x * gain_ref[...]).astype(BF16)
            p = jnp.dot(y, ws_ref[...], preferred_element_type=F32)
            last = jnp.where(lane_all == LANES - 1, ss, p[:, cb:])
            for d in range(ndp):
                at = slice(d * rows, (d + 1) * rows)
                s1[s, d, :, :cb] = p[at, :cb]
                s1[s, d, :, cb:] = last[at]
            for k in range(1, ndp):
                peer = lax.rem(dp + k, ndp)
                send(s1.at[s, peer], r1.at[s, k], sem1.at[s, k], peer, tp)
            width = min(512, lc)
            for c in range(0, 2 * lc, width):
                p = jnp.dot(y, wz_ref[:, c : c + width], preferred_element_type=F32)
                for d in range(ndp):
                    s2[s, d, :, c : c + width] = p[d * rows : (d + 1) * rows]
            for k in range(1, ndp):
                peer = lax.rem(dp + k, ndp)
                send(s2.at[s, peer], r2.at[s, k], sem2.at[s, k], peer, tp)
            for k in range(1, ndp):
                recv(s1.at[s, 0], r1.at[s, k], sem1.at[s, k])
            total = s1[s, dp]
            for k in range(1, ndp):
                total = total + r1[s, k]
            inv = lax.rsqrt(total[:, small - 1 :] / feats + EPS)
            hb[s + 3] = total[:, :cb] * inv
            mixed = convb_ref[4:5, :]
            for i in range(4):
                mixed = mixed + hb[s + i] * convb_ref[i : i + 1, :]
            piece = silu(mixed)
            cs[s] = piece
            cr[s, tp] = piece
            for k in range(1, ntp):
                send(cs.at[s], cr.at[s, tp], c_sem.at[s, k], dp, lax.rem(tp + k, ntp))
            z = total[:, cb:] * inv + dtb_ref[...]
            dt = jnp.maximum(z, 0.0) + jnp.log1p(jnp.exp(-jnp.abs(z)))
            decay = jnp.exp(-dt * rate_ref[...])

            for k in range(1, ndp):
                recv(s2.at[s, 0], r2.at[s, k], sem2.at[s, k])
            inners = []
            for j in range(nchunk):
                at = slice(lc + j * LANES, lc + (j + 1) * LANES)
                here = slice(j * LANES, (j + 1) * LANES)
                v = s2[s, dp, :, at]
                for k in range(1, ndp):
                    v = v + r2[s, k, :, at]
                hx[s + 3, :, here] = v * inv
                mixed = convx_ref[4:5, here]
                for i in range(4):
                    mixed = mixed + hx[s + i, :, here] * convx_ref[i : i + 1, here]
                inner = silu(mixed)
                inners.append(inner)
                dte = jnp.zeros((rows, LANES), F32)
                dece = jnp.zeros((rows, LANES), F32)
                for i in range(hpc):
                    h = j * hpc + i
                    inside = (lane >= i * psize) & (lane < (i + 1) * psize)
                    dte = jnp.where(inside, dt[:, h : h + 1], dte)
                    dece = jnp.where(inside, decay[:, h : h + 1], dece)
                tbuf[j, :rows] = dte * inner
                tbuf[j, rows:] = dece
            for k in range(1, ntp):
                src = lax.rem(tp + ntp - k, ntp)
                recv(cs.at[s], cr.at[s, src], c_sem.at[s, k])
            per = nstate // cb
            b0 = group * nstate // cb
            bmat = [cr[s, b0 + i] for i in range(per)]
            cmat = [cr[s, G * nstate // cb + b0 + i] for i in range(per)]
            bmat = bmat[0] if per == 1 else jnp.concatenate(bmat, axis=1)
            cmat = cmat[0] if per == 1 else jnp.concatenate(cmat, axis=1)
            if s == 0:
                load.wait()

            @pl.loop(0, nchunk)
            def _(j):
                full = jnp.concatenate(
                    [tbuf[j], jnp.zeros((LANES - 2 * rows, LANES), F32)], axis=0
                )
                flipped = full.T
                acc = jnp.zeros((LANES, LANES), F32)
                for r in range(rows):
                    new = (
                        flipped[:, rows + r : rows + r + 1] * state[r, j]
                        + flipped[:, r : r + 1] * bmat[r : r + 1, :]
                    )
                    state[r, j] = new
                    q = jnp.sum(new * cmat[r : r + 1, :], axis=1, keepdims=True)
                    acc = jnp.where(lane_sq == r, q, acc)
                rbuf[j] = acc.T[:rows]

            if s == steps - 1:
                store = pltpu.make_async_copy(state, state_out, st_sem)
                store.start()
            ss = jnp.zeros((rows, LANES), F32)
            for j in range(nchunk):
                here = slice(j * LANES, (j + 1) * LANES)
                v = s2[s, dp, :, here]
                for k in range(1, ndp):
                    v = v + r2[s, k, :, here]
                gated = (rbuf[j] + skip_ref[:, here] * inners[j]) * silu(v * inv)
                ss = ss + gated * gated
                gs[s, :, here] = (gated * ng_ref[:, here]).astype(BF16)
            qs[s] = jnp.broadcast_to(jnp.sum(ss, axis=1, keepdims=True), (rows, LANES))
            gr[s, dp] = gs[s]
            qr[s, dp, member] = qs[s]
            for k in range(1, ndp):
                send(gs.at[s], gr.at[s, dp], g_sem.at[s, k], lax.rem(dp + k, ndp), tp)
            for k in range(ndp):
                for m in range(gsz):
                    if k + m > 0:
                        send(
                            qs.at[s], qr.at[s, dp, member], q_sem.at[s, k, m],
                            lax.rem(dp + k, ndp), group * gsz + lax.rem(member + m, gsz),
                        )
            for k in range(ndp):
                src = lax.rem(dp + ndp - k, ndp)
                if k > 0:
                    recv(gs.at[s], gr.at[s, src], g_sem.at[s, k])
                for m in range(gsz):
                    if k + m > 0:
                        frm = lax.rem(member + gsz - m, gsz)
                        recv(qs.at[s], qr.at[s, src, frm], q_sem.at[s, k, m])
            every = jnp.concatenate(
                [gr[s, d].astype(F32) for d in range(ndp)], axis=0
            ).astype(BF16)
            scales = []
            for d in range(ndp):
                sq = qr[s, d, 0]
                for m in range(1, gsz):
                    sq = sq + qr[s, d, m]
                scales.append(lax.rsqrt(sq[:, :1] / (di // G) + EPS))
            scale = jnp.concatenate(scales, axis=0)
            width = max(ac, min(256, dc))
            for c in range(0, dc, width):
                p = jnp.dot(every, wo_ref[:, c : c + width], preferred_element_type=F32) * scale
                for i in range(width // ac):
                    os[s, c // ac + i] = p[:, i * ac : (i + 1) * ac]
            for k in range(1, ntp):
                peer = lax.rem(tp + k, ntp)
                send(os.at[s, peer], orv.at[s, k], o_sem.at[s, k], dp, peer)
            for k in range(1, ntp):
                recv(os.at[s, 0], orv.at[s, k], o_sem.at[s, k])
            total = os[s, tp]
            for k in range(1, ntp):
                total = total + orv[s, k]
            total = total.astype(BF16)
            ags[s] = total
            agr[s, tp] = total
            for k in range(1, ntp):
                send(ags.at[s], agr.at[s, tp], a_sem.at[s, k], dp, lax.rem(tp + k, ntp))
            for k in range(1, ntp):
                src = lax.rem(tp + ntp - k, ntp)
                recv(ags.at[s], agr.at[s, src], a_sem.at[s, k])
            carried = jnp.concatenate([agr[s, t].astype(F32) for t in range(ntp)], axis=1)
            picked = carried[:, :oc]
            for i in range(1, dc // oc):
                picked = jnp.where(half == i, carried[:, i * oc : (i + 1) * oc], picked)
            for d in range(ndp):
                ms[s, d] = picked[d * rows : (d + 1) * rows].astype(BF16)

            @pl.when(owner == dp)
            def _():
                for k in range(1, ndp):
                    peer = lax.rem(dp + k, ndp)
                    pltpu.make_async_remote_copy(
                        src_ref=ms.at[s, peer], dst_ref=mr.at[s], send_sem=m_sem.at[s, 0],
                        recv_sem=m_sem.at[s, 1], device_id=(peer, tp), device_id_type=MESH,
                    ).start()

        store.wait()
        for s in range(steps):
            def final(s=s):
                return pltpu.make_async_remote_copy(
                    src_ref=ms.at[s, 0], dst_ref=mr.at[s], send_sem=m_sem.at[s, 0],
                    recv_sem=m_sem.at[s, 1], device_id=(dp, tp), device_id_type=MESH,
                )

            @pl.when(owner == dp)
            def _():
                out_ref[s] = ms[s, dp]
                for k in range(1, ndp):
                    final().wait_send()

            @pl.when(owner != dp)
            def _():
                final().wait_recv()
                out_ref[s] = mr[s]

        for copy in pending:
            copy.wait_send()

    vm = pltpu.VMEM
    scratch = [
        vm((rows, nchunk, LANES, nstate), F32),
        vm((steps + 3, rows, lc), F32),
        vm((steps + 3, rows, cb), F32),
        vm((ndp, steps, rows, dc), BF16),
        vm((steps, ndp, rows, small), F32),
        vm((steps, ndp, rows, small), F32),
        vm((steps, ndp, rows, 2 * lc), F32),
        vm((steps, ndp, rows, 2 * lc), F32),
        vm((steps, rows, cb), F32),
        vm((steps, ntp, rows, cb), F32),
        vm((steps, rows, lc), BF16),
        vm((steps, ndp, rows, lc), BF16),
        vm((steps, rows, LANES), F32),
        vm((steps, ndp, gsz, rows, LANES), F32),
        vm((steps, ntp, ndp * rows, ac), F32),
        vm((steps, ntp, ndp * rows, ac), F32),
        vm((steps, ndp * rows, ac), BF16),
        vm((steps, ntp, ndp * rows, ac), BF16),
        vm((steps, ndp, rows, oc), BF16),
        vm((steps, rows, oc), BF16),
        vm((nchunk, 2 * rows, LANES), F32),
        vm((nchunk, rows, LANES), F32),
        pltpu.SemaphoreType.DMA(()),
        pltpu.SemaphoreType.DMA(()),
        pltpu.SemaphoreType.DMA((ndp,)),
        pltpu.SemaphoreType.DMA((steps, ndp)),
        pltpu.SemaphoreType.DMA((steps, ndp)),
        pltpu.SemaphoreType.DMA((steps, ntp)),
        pltpu.SemaphoreType.DMA((steps, ndp)),
        pltpu.SemaphoreType.DMA((steps, ndp, gsz)),
        pltpu.SemaphoreType.DMA((steps, ntp)),
        pltpu.SemaphoreType.DMA((steps, ntp)),
        pltpu.SemaphoreType.DMA((steps, 2)),
    ]
    vspec = pl.BlockSpec(memory_space=pltpu.VMEM)
    hspec = pl.BlockSpec(memory_space=pl.ANY)
    return pl.pallas_call(
        kernel,
        out_shape=(
            jax.ShapeDtypeStruct((steps, rows, oc), BF16),
            jax.ShapeDtypeStruct((rows, nchunk, LANES, nstate), F32),
        ),
        in_specs=[vspec] * 13 + [hspec],
        out_specs=(vspec, hspec),
        scratch_shapes=scratch,
        compiler_params=pltpu.CompilerParams(
            collective_id=0, has_side_effects=True, vmem_limit_bytes=48 * 1024 * 1024
        ),
    )


def body(
    hidden_in, pre_gain, w_zx, zx_codes, zx_exponents, w_bc, w_dt, conv_x, conv_bc, dt_bias,
    decay_rate, skip_gain, conv_state_x, conv_state_bc, ssm_state, norm_gain, w_out, out_codes,
    out_exponents,
):
    ndp, ntp = lax.axis_size("dp"), lax.axis_size("tp")
    dp = lax.axis_index("dp")
    steps, rows, feats = hidden_in.shape
    dc = feats // ndp
    lc = w_zx.shape[2]
    cb = w_bc.shape[1]
    _, heads, psize, nstate = ssm_state.shape
    gsz = ntp // G
    di = lc * ntp

    def mine(a):
        return lax.dynamic_slice_in_dim(a, dp * dc, dc, 0)

    traded = lax.all_to_all(zx_codes, "tp", split_axis=2, concat_axis=0, tiled=True)
    delta = decode_pairs(traded, zx_exponents, BLK)
    wz = (mine(w_zx).astype(F32) + delta).astype(BF16).reshape(dc, 2 * lc)
    wo = (
        lax.dynamic_slice_in_dim(w_out, dp * dc, dc, 1).astype(F32)
        + decode_matrix(out_codes, out_exponents, BLK)
    ).astype(BF16)
    ws = jnp.concatenate(
        [mine(w_bc), jnp.pad(mine(w_dt), ((0, 0), (0, LANES - heads)))], axis=1
    )
    hid = hidden_in.reshape(steps, rows, ndp, dc).transpose(2, 0, 1, 3)

    def padded(a):
        return jnp.pad(a, (0, LANES - heads))[None]

    call = make_kernel(ndp, ntp, steps, rows, dc, lc, cb, heads, psize, nstate, gsz, feats, di)
    out, state = call(
        hid, mine(pre_gain)[None], wz, ws, wo, conv_x, conv_bc, padded(dt_bias),
        padded(decay_rate), jnp.repeat(skip_gain, psize)[None], norm_gain[None],
        conv_state_x.transpose(1, 0, 2), conv_state_bc.transpose(1, 0, 2),
        ssm_state.reshape(rows, lc // LANES, LANES, nstate),
    )
    return out, state.reshape(ssm_state.shape)


def solution(mesh):
    return jax.shard_map(
        body,
        mesh=mesh,
        in_specs=(
            P(None, "dp", None),
            P(),
            P(None, None, "tp"),
            P(("dp", "tp"), None, None),
            P("dp", None, "tp"),
            P(None, "tp"),
            P(None, "tp"),
            P(None, "tp"),
            P(None, "tp"),
            P("tp"),
            P("tp"),
            P("tp"),
            P("dp", None, "tp"),
            P("dp", None, "tp"),
            P("dp", "tp", None, None),
            P("tp"),
            P("tp", None),
            P("tp", "dp"),
            P("tp", "dp"),
        ),
        out_specs=(P(None, "dp", "tp"), P("dp", "tp", None, None)),
        check_vma=False,
    )
```

time: 721 us -> 294 us (0.41)
  blocking collectives: 224 us -> 0 us
  waiting for transfers between devices: 210 us -> 72.6 us
  Pallas kernels: 0 us -> 130 us
  matrix products: 113 us -> 0 us
  other arithmetic: 63.1 us -> 20.1 us
  local copies, waits for them, and re-layouts: 81.8 us -> 62.3 us
  between operations: 14.8 us -> 0.83 us
    psum x8 -> x0, blocking collectives: 167 us -> none  [the longest x4 109 us: body(): whole = lax.psum(partial_value, 'tp').astype(jnp.bfloat16)]
    all_gather x2 -> x0, waiting for transfers between devices: 131 us -> none  [the longest x1 131 us: body(): lax.all_gather(zx_delta.astype(jnp.bfloat16), 'dp', axis=0, tiled=True)]
    pallas_call x0 -> x1, Pallas kernels: none -> 130 us  [body(): call(hid, mine(pre_gain)[None], wz, ws, wo, conv_x, conv_bc, padded(dt_bi...]
    dot_general x20 -> x0, matrix products: 113 us -> none  [the longest x4 51.1 us: body(): jnp.einsum('rhpn,rn->rhp', state, c_group, precision=lax.Precision.HIGHEST)]
    all_gather x4 -> x0, blocking collectives: 56.3 us -> none  [body(): bc_all = lax.all_gather(conv_piece, 'tp', axis=1, tiled=True)]
    convert_element_type x11 -> x3, other arithmetic: 51.2 us -> 20 us  [the longest x1 8.47 us: decode_pairs(): codes.astype(F32).reshape(rows // block, block, pair, cols // block, block)]
    dot_general x1 -> x0, local copies, waits for them, and re-layouts: 20.7 us -> none  [body(): zx = jnp.dot(normed, zx_weights, preferred_element_type=jnp.float32)]
    add x1 -> x0, other arithmetic: 7.69 us -> none  [body(): decay[:, :, None, None] * state]
  transfers between devices with their start and end apart: 3 -> 1, of which waited for: 2 -> 1; matrix products, arithmetic and copies ran while one was open for 11% -> 7% of each run, Pallas kernels for 0% -> 0%
where the time goes in v1:
time: 294 us; the launch traced here: 292 us
  Pallas kernels  130 us (44%)
  waiting for transfers between devices  72.6 us (25%)
  local copies, waits for them, and re-layouts  62.3 us (21%)
  other arithmetic  20.1 us (7%)
  starting transfers between devices  6.49 us (2%)
    pallas_call x1, Pallas kernels, body(): call(hid, mine(pre_gain)[None], wz, ws, wo, conv_x, conv_bc, padded(dt_bi...  130 us
    all_to_all x1, waiting for transfers between devices, body(): lax.all_to_all(zx_codes, 'tp', split_axis=2, concat_axis=0, tiled=True)  72.6 us
    unnamed x33, local copies, waits for them, and re-layouts  28.3 us
    convert_element_type x1, local copies, waits for them, and re-layouts, decode_pairs(): codes.astype(F32).reshape(rows // block, block, pair, cols // block, block)  17 us
    mul x2, local copies, waits for them, and re-layouts, decode_pairs(): return (blocked * scales[:, None, :, :, None]).reshape(rows, pair, cols)  14.9 us
    convert_element_type x1, other arithmetic, decode_pairs(): codes.astype(F32).reshape(rows // block, block, pair, cols // block, block)  8.47 us
    convert_element_type x1, other arithmetic, body(): wz = (mine(w_zx).astype(F32) + delta).astype(BF16).reshape(dc, 2 * lc)  8.37 us
    all_to_all x1, starting transfers between devices, body(): lax.all_to_all(zx_codes, 'tp', split_axis=2, concat_axis=0, tiled=True)  6.49 us
  transfers between devices with their start and end apart: 1, of which 1 were waited for; matrix products, arithmetic and copies ran while one was open for 7% of the time, Pallas kernels for 0%

profile of v1, /device:TPU:0, one launch (start us, length us, event | category | flops | bytes accessed | tf_op | source)
XLA Modules:
  0.0 292.1 jit_solution(10321263658210614336)
XLA Ops:
  0.6 0.0 copy-start
  0.6 15.0 %copy.31 = bf16[128,2,8192]{0,1,2:T(2,128)(2,1)} copy(bf16[128,2,8192]{2,1,0:T(2,128)(2,1)} %param.22) | data formatting | bytes 8388608 | tf_op args[3]
  15.6 0.0 copy-start.8
  15.6 0.0 copy-start.9
  15.6 6.5 %all-to-all-start = ((bf16[128,2,8192]{0,1,2:T(2,128)(2,1)}), bf16[128,2,8192]{0,1,2:T(2,128)(2,1)}, u32[]{:S(2)}, u32[]{:S(2)}) async-start(bf16[128,2,8192]{0,1,2:T(2,128)(2,1)} %copy.31), calls=%async_computation | async-start | bytes 8388608 | tf_op jit(solution)/shard_map/all_to_all | solution.py:367
  22.1 0.0 copy-done.8
  22.1 0.0 copy-done.9
  22.2 4.0 %mul.30 = f32[8,128,2,8,128]{4,3,2,1,0:T(8,128)} broadcast(f32[8,2,8]{2,1,0:T(2,128)S(1)} %multiply_exponential_fusion), dimensions={0,2,3} | broadcast | bytes 8389120 | tf_op jit(solution)/shard_map/mul | solution.py:21
  26.2 0.0 copy-start.11
  26.2 0.0 copy-start.12
  26.2 0.0 copy-start.13
  26.2 0.0 copy-start.10
  26.2 10.9 %mul.31 = f32[1024,2,1024]{2,1,0:T(2,128)} reshape(f32[8,128,2,8,128]{4,3,2,1,0:T(8,128)} %mul.30) | data formatting | bytes 16777216 | tf_op jit(solution)/shard_map/mul | solution.py:21
  37.0 0.7 dynamic_slice.15
  37.7 0.8 constant_dynamic-slice_fusion
  38.5 0.2 copy.34
  38.7 0.0 copy-done.11
  38.7 0.1 broadcast_in_dim.20
  38.7 0.1 broadcast_in_dim_reshape.3.skip_ref
  38.8 0.0 copy-done.12
  38.8 0.0 copy-done.13
  38.8 0.0 copy-start.7
  38.8 0.0 copy-done
  38.9 0.1 fusion.5.ws_ref
  39.0 0.0 copy-done.10
  39.0 0.3 mul.33
  39.4 1.1 copy-done.7
  40.4 3.1 %fusion.3.wo_ref = bf16[1024,1024]{1,0:T(8,128)(2,1)S(1)} fusion(f32[128,8,8,128]{3,2,1,0:T(8,128)S(1)} %bitcast.45, bf16[1024,1024]{1,0:T(8,128)(2,1)S(1)} %copy-done.7, bf16[1024,4096]{1,0:T(8,128)(2,1)} %param.35, s32[]{:T(128)S(6)} %select_n.2), kind=kLoop, calls=%fused_computation.6 | loop fusion | flops 5242880 | bytes 10485764 | tf_op jit(solution)/shard_map/convert_element_type | solution.py:373
  43.6 72.6 %all-to-all-done = bf16[128,2,8192]{0,1,2:T(2,128)(2,1)} async-done(((bf16[128,2,8192]{0,1,2:T(2,128)(2,1)}), bf16[128,2,8192]{0,1,2:T(2,128)(2,1)}, u32[]{:S(2)}, u32[]{:S(2)}) %all-to-all-start) | async-done | bytes 4194336 | tf_op jit(solution)/shard_map/all_to_all | solution.py:367
  116.2 8.5 %convert_bitcast_fusion = f32[8,128,2,1024]{1,2,3,0:T(2,128)} fusion(bf16[128,2,8,1024]{0,1,3,2:T(2,128)(2,1)} %bitcast.12), kind=kLoop, calls=%fused_computation | loop fusion | flops 2097152 | bytes 12582912 | tf_op jit(solution)/shard_map/convert_element_type | solution.py:19
  124.6 17.0 %copy.32 = f32[8,128,2,1024]{3,2,1,0:T(2,128)} copy(f32[8,128,2,1024]{1,2,3,0:T(2,128)} %convert_bitcast_fusion) | data formatting | bytes 16777216 | tf_op jit(solution)/shard_map/convert_element_type | solution.py:19
  141.7 8.4 %fusion.1 = bf16[1024,2,1024]{2,1,0:T(2,128)(2,1)S(1)} fusion(f32[1024,2,1024]{2,1,0:T(2,128)} %mul.31, f32[8,128,2,1024]{3,2,1,0:T(2,128)} %copy.32, bf16[4096,2,1024]{2,1,0:T(2,128)(2,1)} %param.21, s32[]{:T(128)S(6)} %select_n.2), kind=kLoop, calls=%fused_computation.3 | loop fusion | flops 8388608 | bytes 25165828 | tf_op jit(solution)/shard_map/convert_element_type | solution.py:369
  150.1 0.0 copy-start.2
  150.1 0.0 copy-start.3
  150.1 0.0 copy-start.4
  150.1 0.0 copy-start.5
  150.1 0.0 copy-start.6
  150.1 3.4 %copy.36 = bf16[128,8,2,1024]{3,1,2,0:T(8,128)(2,1)} copy(bf16[128,8,2,1024]{3,2,1,0:T(2,128)(2,1)S(1)} %bitcast.46) | data formatting | bytes 8388608
  153.6 0.0 copy-done.2
  153.6 0.0 copy-done.3
  153.6 0.0 copy-done.4
  153.6 0.0 copy-done.5
  153.6 0.0 copy-done.6
  153.6 129.9 %shard_map.194 = (bf16[4,8,512]{2,1,0:T(8,128)(2,1)S(1)}, f32[8,8,128,256]{3,2,1,0:T(8,128)}) custom-call(bf16[4,4,8,1024]{3,2,1,0:T(8,128)(2,1)S(1)} %bitcast.39, f32[1,1024]{1,0:T(1,128)S(1)} %bitcast.41, bf16[1024,2048]{1,0:T(8,128)(2,1)} %bitcast.44, bf16[1024,384]{1,0:T(8,128)(2,1)S(1)} %fusion.5.ws_ref, bf16[1024,1024]{1,0:T(8,128)(2,1)S(1)} %fusion.3.wo_ref, ...), custom_call_target="tpu_custom_call" | custom-call | tf_op jit(solution)/shard_map/pallas_call | solution.py:383
  283.5 0.6 copy.43
  284.1 0.0 copy-start.1
  284.1 8.0 %copy.44 = f32[8,16,64,256]{3,2,1,0:T(8,128)} copy(f32[8,16,64,256]{3,2,1,0:T(8,128)} %bitcast.48) | data formatting | bytes 16777216
  292.1 0.0 copy-done.1
  (5 shorter events, 0.1 us)
Async XLA Ops:
  0.6 38.2 %copy-start = (bf16[4096,256]{1,0:T(8,128)(2,1)S(1)}, bf16[4096,256]{1,0:T(8,128)(2,1)}, u32[]{:S(2)}) copy-start(bf16[4096,256]{1,0:T(8,128)(2,1)} %param.24) | copy-start | bytes 6291460
  15.6 6.5 %copy-start.8 = (bf16[4,8,4096]{2,1,0:T(8,128)(2,1)S(1)}, bf16[4,8,4096]{2,1,0:T(8,128)(2,1)}, u32[]{:S(2)}) copy-start(bf16[4,8,4096]{2,1,0:T(8,128)(2,1)} %param.19) | copy-start | bytes 786436
  15.6 6.5 %copy-start.9 = (s32[8,2,8]{2,1,0:T(2,128)S(1)}, s32[8,2,8]{2,1,0:T(2,128)}, u32[]{:S(2)}) copy-start(s32[8,2,8]{2,1,0:T(2,128)} %param.23) | copy-start | bytes 1540
  15.6 100.6 %all-to-all-start = ((bf16[128,2,8192]{0,1,2:T(2,128)(2,1)}), bf16[128,2,8192]{0,1,2:T(2,128)(2,1)}, u32[]{:S(2)}, u32[]{:S(2)}) async-start(bf16[128,2,8192]{0,1,2:T(2,128)(2,1)} %copy.31), calls=%async_computation | async-start | bytes 8388608 | tf_op jit(solution)/shard_map/all_to_all | solution.py:367
  26.2 12.5 %copy-start.11 = (f32[16]{0:T(128)S(1)}, f32[16]{0:T(128)}, u32[]{:S(2)}) copy-start(f32[16]{0:T(128)} %param.30) | copy-start | bytes 196
  26.2 12.7 %copy-start.12 = (f32[16]{0:T(128)S(1)}, f32[16]{0:T(128)}, u32[]{:S(2)}) copy-start(f32[16]{0:T(128)} %param.29) | copy-start | bytes 196
  26.2 12.7 %copy-start.13 = (f32[16]{0:T(128)S(1)}, f32[16]{0:T(128)}, u32[]{:S(2)}) copy-start(f32[16]{0:T(128)} %param.28) | copy-start | bytes 196
  26.2 12.8 %copy-start.10 = (s32[8,8]{1,0:T(8,128)S(1)}, s32[8,8]{1,0:T(8,128)}, u32[]{:S(2)}) copy-start(s32[8,8]{1,0:T(8,128)} %param.37) | copy-start | bytes 772
  38.8 1.6 copy-start.7
  150.1 3.5 %copy-start.2 = (bf16[8,3,1024]{2,0,1:T(8,128)(2,1)S(1)}, bf16[8,3,1024]{2,0,1:T(8,128)(2,1)}, u32[]{:S(2)}) copy-start(bf16[8,3,1024]{2,0,1:T(8,128)(2,1)} %param.31) | copy-start | bytes 147460
  150.1 3.5 %copy-start.3 = (f32[5,1024]{1,0:T(8,128)S(1)}, f32[5,1024]{1,0:T(8,128)}, u32[]{:S(2)}) copy-start(f32[5,1024]{1,0:T(8,128)} %convx_ref.1) | copy-start | bytes 61444
  150.1 3.5 %copy-start.4 = (bf16[8,3,256]{2,0,1:T(8,128)(2,1)S(1)}, bf16[8,3,256]{2,0,1:T(8,128)(2,1)}, u32[]{:S(2)}) copy-start(bf16[8,3,256]{2,0,1:T(8,128)(2,1)} %param.32) | copy-start | bytes 36868
  150.1 3.5 %copy-start.5 = (f32[5,256]{1,0:T(8,128)S(1)}, f32[5,256]{1,0:T(8,128)}, u32[]{:S(2)}) copy-start(f32[5,256]{1,0:T(8,128)} %convb_ref.1) | copy-start | bytes 15364
  150.1 3.5 %copy-start.6 = (f32[1024]{0:T(1024)S(1)}, f32[1024]{0:T(1024)}, u32[]{:S(2)}) copy-start(f32[1024]{0:T(1024)} %param.34) | copy-start | bytes 12292
  284.1 8.0 %copy-start.1 = (bf16[4096,256]{1,0:T(8,128)(2,1)S(1)}, bf16[4096,256]{1,0:T(8,128)(2,1)}, u32[]{:S(2)}) copy-start(bf16[4096,256]{1,0:T(8,128)(2,1)} %param.24) | copy-start | bytes 6291460

commit v2 on v1

--- a/solution.py
+++ b/solution.py
@@ -14,20 +14,6 @@
 BF16 = jnp.bfloat16
 
 
-def decode_pairs(codes, exponents, block):
-    rows, pair, cols = codes.shape
-    blocked = codes.astype(F32).reshape(rows // block, block, pair, cols // block, block)
-    scales = jnp.exp2(exponents.astype(F32))
-    return (blocked * scales[:, None, :, :, None]).reshape(rows, pair, cols)
-
-
-def decode_matrix(codes, exponents, block):
-    rows, cols = codes.shape
-    blocked = codes.astype(F32).reshape(rows // block, block, cols // block, block)
-    scales = jnp.exp2(exponents.astype(F32))
-    return (blocked * scales[:, None, :, None]).reshape(rows, cols)
-
-
 def silu(v):
     return v / (1.0 + jnp.exp(-v))
 
@@ -38,14 +24,15 @@
     nchunk = lc // LANES
     hpc = LANES // psize
     small = cb + LANES
+    rpd = dc // ntp
 
     def kernel(
-        hid_ref, gain_ref, wz_ref, ws_ref, wo_ref, convx_ref, convb_ref, dtb_ref, rate_ref,
-        skip_ref, ng_ref, hx0_ref, hb0_ref, state_hbm,
+        hid_ref, gain_ref, wdt_ref, sc_ref, so_ref, ocodes_ref, convx_ref, convb_ref, dtb_ref, rate_ref,
+        skip_ref, ng_ref, hx0_ref, hb0_ref, state_hbm, codes_hbm, wzx_hbm, wbc_hbm, wout_hbm,
         out_ref, state_out,
         state, hx, hb, hrecv, s1, r1, s2, r2, cs, cr, gs, gr, qs, qr, os, orv, ags, agr, ms, mr,
-        tbuf, rbuf,
-        st_sem, send_sem, h_sem, sem1, sem2, c_sem, g_sem, q_sem, o_sem, a_sem, m_sem,
+        tbuf, rbuf, rv, wv, wz, wbc, wo,
+        w_sems, v_sem, st_sem, send_sem, h_sem, sem1, sem2, c_sem, g_sem, q_sem, o_sem, a_sem, m_sem,
     ):
         dp = lax.axis_index("dp")
         tp = lax.axis_index("tp")
@@ -66,6 +53,18 @@
             ).wait_recv()
 
         load = pltpu.make_async_copy(state_hbm, state, st_sem)
+        load_w = pltpu.make_async_copy(wzx_hbm.at[pl.ds(dp * dc, dc)], wv, w_sems.at[0])
+        load_w.start()
+        load_own = pltpu.make_async_copy(
+            codes_hbm.at[:, :, pl.ds(pl.multiple_of(tp * lc, LANES), lc)], rv.at[tp], w_sems.at[1]
+        )
+        load_own.start()
+        load_bc = pltpu.make_async_copy(wbc_hbm.at[pl.ds(dp * dc, dc)], wbc, w_sems.at[2])
+        load_bc.start()
+        load_out = pltpu.make_async_copy(
+            wout_hbm.at[:, pl.ds(pl.multiple_of(dp * dc, LANES), dc)], wo, w_sems.at[3]
+        )
+        load_out.start()
         load.start()
 
         barrier = pltpu.get_barrier_semaphore()
@@ -79,6 +78,12 @@
                     )
         pl.semaphore_wait(barrier, ndp * ntp - 1)
 
+        for k in range(ntp - 1, 0, -1):
+            peer = tp ^ k
+            send(
+                codes_hbm.at[:, :, pl.ds(pl.multiple_of(peer * lc, LANES), lc)],
+                rv.at[tp], v_sem.at[k], dp, peer,
+            )
         for k in range(1, ndp):
             peer = lax.rem(dp + k, ndp)
             send(hid_ref.at[peer], hrecv.at[dp], h_sem.at[k], peer, tp)
@@ -89,9 +94,35 @@
             src = lax.rem(dp + ndp - k, ndp)
             recv(hid_ref.at[src], hrecv.at[src], h_sem.at[k])
 
+        load_out.wait()
+
+        @pl.loop(0, lc // 32)
+        def _(i):
+            at = pl.ds(pl.multiple_of(i * 32, 32), 32)
+            delta = ocodes_ref[at, :].astype(F32) * so_ref[i // (BLK // 32)]
+            wo[at, :] = (wo[at, :].astype(F32) + delta).astype(BF16)
+
+        load_w.wait()
+        load_own.wait()
+        load_bc.wait()
+        for k in [0] + list(range(ntp - 1, 0, -1)):
+            src = tp ^ k
+            if k > 0:
+                recv(rv.at[src], rv.at[src], v_sem.at[k])
+
+            @pl.loop(0, rpd // 16)
+            def _(i, src=src):
+                first = src * rpd + i * 16
+                code = rv[src, pl.ds(i * 16, 16)].astype(F32)
+                old = wv[pl.ds(first, 16)].astype(F32)
+                new = old + code * sc_ref[src * rpd // BLK][None]
+                wz[pl.ds(pl.multiple_of(2 * first, 32), 32), :] = new.astype(BF16).reshape(32, lc)
+
         lane = lax.broadcasted_iota(jnp.int32, (rows, LANES), 1)
         lane_all = lax.broadcasted_iota(jnp.int32, (ndp * rows, LANES), 1)
         lane_sq = lax.broadcasted_iota(jnp.int32, (LANES, LANES), 1)
+        put_row = lax.broadcasted_iota(jnp.int32, (LANES, 2 * LANES), 0)
+        put_col = lax.broadcasted_iota(jnp.int32, (LANES, 2 * LANES), 1)
         owner = tp * oc // dc
         half = (tp * oc - owner * dc) // oc
         group = tp // gsz
@@ -103,20 +134,33 @@
                 x = x + carried
             ss = jnp.sum(x * x, axis=1, keepdims=True)
             y = (x * gain_ref[...]).astype(BF16)
-            p = jnp.dot(y, ws_ref[...], preferred_element_type=F32)
-            last = jnp.where(lane_all == LANES - 1, ss, p[:, cb:])
+            p = jnp.dot(y, wbc[...], preferred_element_type=F32)
+            last = jnp.dot(y, wdt_ref[...], preferred_element_type=F32)
+            last = jnp.where(lane_all == LANES - 1, ss, last)
             for d in range(ndp):
                 at = slice(d * rows, (d + 1) * rows)
-                s1[s, d, :, :cb] = p[at, :cb]
+                s1[s, d, :, :cb] = p[at]
                 s1[s, d, :, cb:] = last[at]
             for k in range(1, ndp):
                 peer = lax.rem(dp + k, ndp)
                 send(s1.at[s, peer], r1.at[s, k], sem1.at[s, k], peer, tp)
-            width = min(512, lc)
-            for c in range(0, 2 * lc, width):
-                p = jnp.dot(y, wz_ref[:, c : c + width], preferred_element_type=F32)
+            spread = []
+            for half_of in range(2):
+                place = (put_col == 2 * put_row + half_of).astype(BF16)
+                parts = [
+                    jnp.dot(y[:, c : c + LANES], place, preferred_element_type=F32).astype(BF16)
+                    for c in range(0, dc, LANES)
+                ]
+                spread.append(jnp.concatenate(parts, axis=1))
+            spread = jnp.concatenate(spread, axis=0)
+            width = min(256, lc)
+            for c in range(0, lc, width):
+                p = jnp.dot(spread, wz[:, c : c + width], preferred_element_type=F32)
                 for d in range(ndp):
                     s2[s, d, :, c : c + width] = p[d * rows : (d + 1) * rows]
+                    s2[s, d, :, lc + c : lc + c + width] = p[
+                        (ndp + d) * rows : (ndp + d + 1) * rows
+                    ]
             for k in range(1, ndp):
                 peer = lax.rem(dp + k, ndp)
                 send(s2.at[s, peer], r2.at[s, k], sem2.at[s, k], peer, tp)
@@ -236,7 +280,7 @@
             scale = jnp.concatenate(scales, axis=0)
             width = max(ac, min(256, dc))
             for c in range(0, dc, width):
-                p = jnp.dot(every, wo_ref[:, c : c + width], preferred_element_type=F32) * scale
+                p = jnp.dot(every, wo[:, c : c + width], preferred_element_type=F32) * scale
                 for i in range(width // ac):
                     os[s, c // ac + i] = p[:, i * ac : (i + 1) * ac]
             for k in range(1, ntp):
@@ -317,6 +361,13 @@
         vm((steps, rows, oc), BF16),
         vm((nchunk, 2 * rows, LANES), F32),
         vm((nchunk, rows, LANES), F32),
+        vm((ntp, rpd, 2, lc), BF16),
+        vm((dc, 2, lc), BF16),
+        vm((2 * dc, lc), BF16),
+        vm((dc, cb), BF16),
+        vm((lc, dc), BF16),
+        pltpu.SemaphoreType.DMA((4,)),
+        pltpu.SemaphoreType.DMA((ntp,)),
         pltpu.SemaphoreType.DMA(()),
         pltpu.SemaphoreType.DMA(()),
         pltpu.SemaphoreType.DMA((ndp,)),
@@ -337,7 +388,7 @@
             jax.ShapeDtypeStruct((steps, rows, oc), BF16),
             jax.ShapeDtypeStruct((rows, nchunk, LANES, nstate), F32),
         ),
-        in_specs=[vspec] * 13 + [hspec],
+        in_specs=[vspec] * 14 + [hspec] * 5,
         out_specs=(vspec, hspec),
         scratch_shapes=scratch,
         compiler_params=pltpu.CompilerParams(
@@ -364,16 +415,9 @@
     def mine(a):
         return lax.dynamic_slice_in_dim(a, dp * dc, dc, 0)
 
-    traded = lax.all_to_all(zx_codes, "tp", split_axis=2, concat_axis=0, tiled=True)
-    delta = decode_pairs(traded, zx_exponents, BLK)
-    wz = (mine(w_zx).astype(F32) + delta).astype(BF16).reshape(dc, 2 * lc)
-    wo = (
-        lax.dynamic_slice_in_dim(w_out, dp * dc, dc, 1).astype(F32)
-        + decode_matrix(out_codes, out_exponents, BLK)
-    ).astype(BF16)
-    ws = jnp.concatenate(
-        [mine(w_bc), jnp.pad(mine(w_dt), ((0, 0), (0, LANES - heads)))], axis=1
-    )
+    sc = jnp.repeat(jnp.exp2(zx_exponents.astype(F32)), BLK, axis=2)
+    so = jnp.repeat(jnp.exp2(out_exponents.astype(F32)), BLK, axis=1)[:, None]
+    wdt = jnp.pad(mine(w_dt), ((0, 0), (0, LANES - heads)))
     hid = hidden_in.reshape(steps, rows, ndp, dc).transpose(2, 0, 1, 3)
 
     def padded(a):
@@ -381,10 +425,11 @@
 
     call = make_kernel(ndp, ntp, steps, rows, dc, lc, cb, heads, psize, nstate, gsz, feats, di)
     out, state = call(
-        hid, mine(pre_gain)[None], wz, ws, wo, conv_x, conv_bc, padded(dt_bias),
+        hid, mine(pre_gain)[None], wdt, sc, so, out_codes, conv_x, conv_bc, padded(dt_bias),
         padded(decay_rate), jnp.repeat(skip_gain, psize)[None], norm_gain[None],
         conv_state_x.transpose(1, 0, 2), conv_state_bc.transpose(1, 0, 2),
         ssm_state.reshape(rows, lc // LANES, LANES, nstate),
+        zx_codes, w_zx, w_bc, w_out,
     )
     return out, state.reshape(ssm_state.shape)
 

time: 294 us -> 244 us (0.83)
  Pallas kernels: 130 us -> 222 us
  waiting for transfers between devices: 72.6 us -> 0 us
  local copies, waits for them, and re-layouts: 62.3 us -> 18.9 us
  other arithmetic: 20.1 us -> 1.41 us
  starting transfers between devices: 6.49 us -> 0 us
    pallas_call x1, Pallas kernels: 130 us -> 222 us  [body(): call(hid, mine(pre_gain)[None], wdt, sc, so, out_codes, conv_x, conv_bc,...]
    all_to_all x1 -> x0, waiting for transfers between devices: 72.6 us -> none  [body(): lax.all_to_all(zx_codes, 'tp', split_axis=2, concat_axis=0, tiled=True)]
    convert_element_type x3 -> x0, other arithmetic: 20 us -> none  [the longest x1 8.47 us: decode_pairs(): codes.astype(F32).reshape(rows // block, block, pair, cols // block, block)]
    convert_element_type x1 -> x0, local copies, waits for them, and re-layouts: 17 us -> none  [decode_pairs(): codes.astype(F32).reshape(rows // block, block, pair, cols // block, block)]
    mul x3 -> x0, local copies, waits for them, and re-layouts: 15.2 us -> none  [the longest x2 14.9 us: decode_pairs(): return (blocked * scales[:, None, :, :, None]).reshape(rows, pair, cols)]
    unnamed x33 -> x19, local copies, waits for them, and re-layouts: 28.3 us -> 15.5 us
    all_to_all x1 -> x0, starting transfers between devices: 6.49 us -> none  [body(): lax.all_to_all(zx_codes, 'tp', split_axis=2, concat_axis=0, tiled=True)]
  transfers between devices with their start and end apart: 1 -> 0, of which waited for: 1 -> 0; matrix products, arithmetic and copies ran while one was open for 7% -> 0% of each run, Pallas kernels for 0% -> 0%
where the time goes in v2:
time: 244 us; the launch traced here: 243 us
  Pallas kernels  222 us (91%)
  local copies, waits for them, and re-layouts  18.9 us (8%)
    pallas_call x1, Pallas kernels, body(): call(hid, mine(pre_gain)[None], wdt, sc, so, out_codes, conv_x, conv_bc,...  222 us
    unnamed x19, local copies, waits for them, and re-layouts  15.5 us

profile of v2, /device:TPU:0, one launch (start us, length us, event | category | flops | bytes accessed | tf_op | source)
XLA Modules:
  0.0 243.0 jit_solution(14657571816658776705)
XLA Ops:
  0.6 0.0 copy-start
  0.7 0.7 pad_bitcast_fusion
  1.4 0.7 dynamic_slice.6
  2.0 0.7 multiply_exponential_fusion.1
  2.7 0.7 multiply_exponential_fusion
  3.5 0.7 broadcast_in_dim.26
  4.2 0.1 broadcast_in_dim_reshape.7.skip_ref
  4.3 0.1 broadcast_in_dim.23
  4.3 0.0 copy-done
  4.3 0.1 broadcast_in_dim.22
  4.5 0.2 copy.24
  4.6 0.1 pad.11.wdt_ref
  4.7 1.0 copy.27
  5.7 0.0 copy-start.1
  5.7 1.6 copy-done.1
  7.3 0.0 copy-start.2
  7.3 1.6 copy-done.2
  8.9 0.0 copy-start.3
  8.9 0.8 copy-done.3
  9.7 0.0 copy-start.4
  9.7 0.8 copy-done.4
  10.4 0.0 copy-start.5
  10.4 0.7 copy-done.5
  11.1 0.0 copy-start.6
  11.1 0.7 copy-done.6
  11.8 0.0 copy-start.7
  11.8 0.7 copy-done.7
  12.5 222.0 %shard_map.194 = (bf16[4,8,512]{2,1,0:T(8,128)(2,1)S(1)}, f32[8,8,128,256]{3,2,1,0:T(8,128)}) custom-call(bf16[4,4,8,1024]{3,2,1,0:T(8,128)(2,1)S(1)} %bitcast.20, f32[1,1024]{1,0:T(1,128)S(1)} %bitcast.23, bf16[1024,128]{1,0:T(8,128)(2,1)S(1)} %pad.11.wdt_ref, f32[8,2,1024]{2,1,0:T(2,128)S(1)} %reshape.17.sc_ref, f32[8,1,1024]{2,1,0:T(1,128)S(1)} %bitcast.21, ...), custom_call_target="tpu_custom_call" | custom-call | tf_op jit(solution)/shard_map/pallas_call | solution.py:427
  234.5 0.6 copy.30
  235.1 7.9 %copy.31 = f32[8,16,64,256]{3,2,1,0:T(8,128)} copy(f32[8,16,64,256]{3,2,1,0:T(8,128)} %bitcast.26) | data formatting | bytes 16777216
  (2 shorter events, 0.0 us)
Async XLA Ops:
  0.6 3.7 %copy-start = (bf16[4096,16]{0,1:T(8,128)(2,1)S(1)}, bf16[4096,16]{0,1:T(8,128)(2,1)}, u32[]{:S(2)}) copy-start(bf16[4096,16]{0,1:T(8,128)(2,1)} %param.25) | copy-start | bytes 393220
  5.7 1.6 copy-start.1
  7.3 1.6 copy-start.2
  8.9 0.8 copy-start.3
  9.7 0.8 copy-start.4
  10.4 0.7 copy-start.5
  11.1 0.7 copy-start.6
  11.8 0.7 copy-start.7

commit v3 on v2

--- a/solution.py
+++ b/solution.py
@@ -27,11 +27,14 @@
     rpd = dc // ntp
 
     def kernel(
-        hid_ref, gain_ref, wdt_ref, sc_ref, so_ref, ocodes_ref, convx_ref, convb_ref, dtb_ref, rate_ref,
-        skip_ref, ng_ref, hx0_ref, hb0_ref, state_hbm, codes_hbm, wzx_hbm, wbc_hbm, wout_hbm,
+        hid_hbm, gain_hbm, wdt_hbm, sc_hbm, so_hbm, ocodes_hbm, convx_hbm, convb_hbm, dtb_hbm,
+        rate_hbm, skip_hbm, ng_hbm, hx0_hbm, hb0_hbm, state_hbm, codes_hbm, wzx_hbm, wbc_hbm,
+        wout_hbm,
         out_ref, state_out,
         state, hx, hb, hrecv, s1, r1, s2, r2, cs, cr, gs, gr, qs, qr, os, orv, ags, agr, ms, mr,
         tbuf, rbuf, rv, wv, wz, wbc, wo,
+        gain_ref, wdt_in, wdt_ref, sc_in, sc_ref, so_in, so_ref, ocodes_ref, convx_ref, convb_ref,
+        dtb_ref, rate_ref, skip_ref, ng_ref, hx0_ref, hb0_ref, l_sems,
         w_sems, v_sem, st_sem, send_sem, h_sem, sem1, sem2, c_sem, g_sem, q_sem, o_sem, a_sem, m_sem,
     ):
         dp = lax.axis_index("dp")
@@ -67,6 +70,22 @@
         load_out.start()
         load.start()
 
+        def chunk(i):
+            return pl.ds(pl.multiple_of(i * dc, LANES), dc)
+
+        small_loads = [
+            (gain_hbm.at[:, chunk(dp)], gain_ref), (wdt_hbm.at[:, chunk(dp)], wdt_in),
+            (sc_hbm, sc_in), (so_hbm, so_in), (ocodes_hbm, ocodes_ref), (convx_hbm, convx_ref),
+            (convb_hbm, convb_ref), (dtb_hbm, dtb_ref), (rate_hbm, rate_ref),
+            (skip_hbm, skip_ref), (ng_hbm, ng_ref), (hx0_hbm, hx0_ref), (hb0_hbm, hb0_ref),
+            (hid_hbm.at[:, :, chunk(dp)], hrecv.at[dp]),
+        ]
+        small_loads = [
+            pltpu.make_async_copy(a, b, l_sems.at[i]) for i, (a, b) in enumerate(small_loads)
+        ]
+        for copy in small_loads:
+            copy.start()
+
         barrier = pltpu.get_barrier_semaphore()
         for i in range(ndp):
             for j in range(ntp):
@@ -86,13 +105,28 @@
             )
         for k in range(1, ndp):
             peer = lax.rem(dp + k, ndp)
-            send(hid_ref.at[peer], hrecv.at[dp], h_sem.at[k], peer, tp)
-        hrecv[dp] = hid_ref[dp]
+            send(hid_hbm.at[:, :, chunk(peer)], hrecv.at[dp], h_sem.at[k], peer, tp)
+        for copy in small_loads:
+            copy.wait()
+        wdt_ref[...] = jnp.concatenate(
+            [wdt_in[...].astype(F32), jnp.zeros((LANES - heads, dc), F32)], axis=0
+        ).astype(BF16)
+        for ref, table in ((sc_in, sc_ref), (so_in, so_ref)):
+            power = jnp.exp2(ref[...].astype(F32))
+            nrow, pair, ncol = power.shape
+            for b in range(nrow):
+                table[b] = jnp.concatenate(
+                    [
+                        jnp.broadcast_to(power[b, :, c : c + 1], (pair, BLK))
+                        for c in range(ncol)
+                    ],
+                    axis=1,
+                )
         hx[0:3] = hx0_ref[...].astype(F32)
         hb[0:3] = hb0_ref[...].astype(F32)
         for k in range(1, ndp):
             src = lax.rem(dp + ndp - k, ndp)
-            recv(hid_ref.at[src], hrecv.at[src], h_sem.at[k])
+            recv(hrecv.at[src], hrecv.at[src], h_sem.at[k])
 
         load_out.wait()
 
@@ -135,7 +169,9 @@
             ss = jnp.sum(x * x, axis=1, keepdims=True)
             y = (x * gain_ref[...]).astype(BF16)
             p = jnp.dot(y, wbc[...], preferred_element_type=F32)
-            last = jnp.dot(y, wdt_ref[...], preferred_element_type=F32)
+            last = lax.dot_general(
+                y, wdt_ref[...], (((1,), (1,)), ((), ())), preferred_element_type=F32
+            )
             last = jnp.where(lane_all == LANES - 1, ss, last)
             for d in range(ndp):
                 at = slice(d * rows, (d + 1) * rows)
@@ -157,10 +193,10 @@
             for c in range(0, lc, width):
                 p = jnp.dot(spread, wz[:, c : c + width], preferred_element_type=F32)
                 for d in range(ndp):
-                    s2[s, d, :, c : c + width] = p[d * rows : (d + 1) * rows]
+                    s2[s, d, :, c : c + width] = p[d * rows : (d + 1) * rows].astype(BF16)
                     s2[s, d, :, lc + c : lc + c + width] = p[
                         (ndp + d) * rows : (ndp + d + 1) * rows
-                    ]
+                    ].astype(BF16)
             for k in range(1, ndp):
                 peer = lax.rem(dp + k, ndp)
                 send(s2.at[s, peer], r2.at[s, k], sem2.at[s, k], peer, tp)
@@ -179,7 +215,7 @@
             cr[s, tp] = piece
             for k in range(1, ntp):
                 send(cs.at[s], cr.at[s, tp], c_sem.at[s, k], dp, lax.rem(tp + k, ntp))
-            z = total[:, cb:] * inv + dtb_ref[...]
+            z = total[:, cb : cb + heads] * inv + dtb_ref[...]
             dt = jnp.maximum(z, 0.0) + jnp.log1p(jnp.exp(-jnp.abs(z)))
             decay = jnp.exp(-dt * rate_ref[...])
 
@@ -189,22 +225,24 @@
             for j in range(nchunk):
                 at = slice(lc + j * LANES, lc + (j + 1) * LANES)
                 here = slice(j * LANES, (j + 1) * LANES)
-                v = s2[s, dp, :, at]
+                v = s2[s, dp, :, at].astype(F32)
                 for k in range(1, ndp):
-                    v = v + r2[s, k, :, at]
+                    v = v + r2[s, k, :, at].astype(F32)
                 hx[s + 3, :, here] = v * inv
                 mixed = convx_ref[4:5, here]
                 for i in range(4):
                     mixed = mixed + hx[s + i, :, here] * convx_ref[i : i + 1, here]
                 inner = silu(mixed)
-                inners.append(inner)
                 dte = jnp.zeros((rows, LANES), F32)
                 dece = jnp.zeros((rows, LANES), F32)
+                skip = jnp.zeros((rows, LANES), F32)
                 for i in range(hpc):
                     h = j * hpc + i
                     inside = (lane >= i * psize) & (lane < (i + 1) * psize)
                     dte = jnp.where(inside, dt[:, h : h + 1], dte)
                     dece = jnp.where(inside, decay[:, h : h + 1], dece)
+                    skip = jnp.where(inside, skip_ref[:, h : h + 1], skip)
+                inners.append(skip * inner)
                 tbuf[j, :rows] = dte * inner
                 tbuf[j, rows:] = dece
             for k in range(1, ntp):
@@ -242,10 +280,10 @@
             ss = jnp.zeros((rows, LANES), F32)
             for j in range(nchunk):
                 here = slice(j * LANES, (j + 1) * LANES)
-                v = s2[s, dp, :, here]
+                v = s2[s, dp, :, here].astype(F32)
                 for k in range(1, ndp):
-                    v = v + r2[s, k, :, here]
-                gated = (rbuf[j] + skip_ref[:, here] * inners[j]) * silu(v * inv)
+                    v = v + r2[s, k, :, here].astype(F32)
+                gated = (rbuf[j] + inners[j]) * silu(v * inv)
                 ss = ss + gated * gated
                 gs[s, :, here] = (gated * ng_ref[:, here]).astype(BF16)
             qs[s] = jnp.broadcast_to(jnp.sum(ss, axis=1, keepdims=True), (rows, LANES))
@@ -282,15 +320,15 @@
             for c in range(0, dc, width):
                 p = jnp.dot(every, wo[:, c : c + width], preferred_element_type=F32) * scale
                 for i in range(width // ac):
-                    os[s, c // ac + i] = p[:, i * ac : (i + 1) * ac]
+                    os[s, c // ac + i] = p[:, i * ac : (i + 1) * ac].astype(BF16)
             for k in range(1, ntp):
                 peer = lax.rem(tp + k, ntp)
                 send(os.at[s, peer], orv.at[s, k], o_sem.at[s, k], dp, peer)
             for k in range(1, ntp):
                 recv(os.at[s, 0], orv.at[s, k], o_sem.at[s, k])
-            total = os[s, tp]
-            for k in range(1, ntp):
-                total = total + orv[s, k]
+            total = os[s, tp].astype(F32)
+            for k in range(1, ntp):
+                total = total + orv[s, k].astype(F32)
             total = total.astype(BF16)
             ags[s] = total
             agr[s, tp] = total
@@ -345,16 +383,16 @@
         vm((ndp, steps, rows, dc), BF16),
         vm((steps, ndp, rows, small), F32),
         vm((steps, ndp, rows, small), F32),
-        vm((steps, ndp, rows, 2 * lc), F32),
-        vm((steps, ndp, rows, 2 * lc), F32),
+        vm((steps, ndp, rows, 2 * lc), BF16),
+        vm((steps, ndp, rows, 2 * lc), BF16),
         vm((steps, rows, cb), F32),
         vm((steps, ntp, rows, cb), F32),
         vm((steps, rows, lc), BF16),
         vm((steps, ndp, rows, lc), BF16),
         vm((steps, rows, LANES), F32),
         vm((steps, ndp, gsz, rows, LANES), F32),
-        vm((steps, ntp, ndp * rows, ac), F32),
-        vm((steps, ntp, ndp * rows, ac), F32),
+        vm((steps, ntp, ndp * rows, ac), BF16),
+        vm((steps, ntp, ndp * rows, ac), BF16),
         vm((steps, ndp * rows, ac), BF16),
         vm((steps, ntp, ndp * rows, ac), BF16),
         vm((steps, ndp, rows, oc), BF16),
@@ -366,6 +404,23 @@
         vm((2 * dc, lc), BF16),
         vm((dc, cb), BF16),
         vm((lc, dc), BF16),
+        vm((1, dc), F32),
+        vm((heads, dc), BF16),
+        vm((LANES, dc), BF16),
+        vm((dc // BLK, 2, lc // BLK), jnp.int32),
+        vm((dc // BLK, 2, lc), F32),
+        vm((lc // BLK, 1, dc // BLK), jnp.int32),
+        vm((lc // BLK, 1, dc), F32),
+        vm((lc, dc), BF16),
+        vm((5, lc), F32),
+        vm((5, cb), F32),
+        vm((1, heads), F32),
+        vm((1, heads), F32),
+        vm((1, heads), F32),
+        vm((1, lc), F32),
+        vm((3, rows, lc), BF16),
+        vm((3, rows, cb), BF16),
+        pltpu.SemaphoreType.DMA((14,)),
         pltpu.SemaphoreType.DMA((4,)),
         pltpu.SemaphoreType.DMA((ntp,)),
         pltpu.SemaphoreType.DMA(()),
@@ -388,11 +443,11 @@
             jax.ShapeDtypeStruct((steps, rows, oc), BF16),
             jax.ShapeDtypeStruct((rows, nchunk, LANES, nstate), F32),
         ),
-        in_specs=[vspec] * 14 + [hspec] * 5,
+        in_specs=[hspec] * 19,
         out_specs=(vspec, hspec),
         scratch_shapes=scratch,
         compiler_params=pltpu.CompilerParams(
-            collective_id=0, has_side_effects=True, vmem_limit_bytes=48 * 1024 * 1024
+            collective_id=0, has_side_effects=True, vmem_limit_bytes=60 * 1024 * 1024
         ),
     )
 
@@ -403,7 +458,6 @@
     out_exponents,
 ):
     ndp, ntp = lax.axis_size("dp"), lax.axis_size("tp")
-    dp = lax.axis_index("dp")
     steps, rows, feats = hidden_in.shape
     dc = feats // ndp
     lc = w_zx.shape[2]
@@ -412,21 +466,10 @@
     gsz = ntp // G
     di = lc * ntp
 
-    def mine(a):
-        return lax.dynamic_slice_in_dim(a, dp * dc, dc, 0)
-
-    sc = jnp.repeat(jnp.exp2(zx_exponents.astype(F32)), BLK, axis=2)
-    so = jnp.repeat(jnp.exp2(out_exponents.astype(F32)), BLK, axis=1)[:, None]
-    wdt = jnp.pad(mine(w_dt), ((0, 0), (0, LANES - heads)))
-    hid = hidden_in.reshape(steps, rows, ndp, dc).transpose(2, 0, 1, 3)
-
-    def padded(a):
-        return jnp.pad(a, (0, LANES - heads))[None]
-
     call = make_kernel(ndp, ntp, steps, rows, dc, lc, cb, heads, psize, nstate, gsz, feats, di)
     out, state = call(
-        hid, mine(pre_gain)[None], wdt, sc, so, out_codes, conv_x, conv_bc, padded(dt_bias),
-        padded(decay_rate), jnp.repeat(skip_gain, psize)[None], norm_gain[None],
+        hidden_in, pre_gain[None], w_dt.T, zx_exponents, out_exponents[:, None], out_codes, conv_x,
+        conv_bc, dt_bias[None], decay_rate[None], skip_gain[None], norm_gain[None],
         conv_state_x.transpose(1, 0, 2), conv_state_bc.transpose(1, 0, 2),
         ssm_state.reshape(rows, lc // LANES, LANES, nstate),
         zx_codes, w_zx, w_bc, w_out,

time: 244 us -> 230 us (0.943)
  local copies, waits for them, and re-layouts: 18.9 us -> 9.27 us
  Pallas kernels: 222 us -> 219 us
    unnamed x19 -> x2, local copies, waits for them, and re-layouts: 15.5 us -> 9.27 us
    pallas_call x1, Pallas kernels: 222 us -> 219 us  [body(): call(hidden_in, pre_gain[None], w_dt.T, zx_exponents, out_exponents[:, No...]
where the time goes in v3:
time: 230 us; the launch traced here: 229 us
  Pallas kernels  219 us (95%)
  local copies, waits for them, and re-layouts  9.27 us (4%)
    pallas_call x1, Pallas kernels, body(): call(hidden_in, pre_gain[None], w_dt.T, zx_exponents, out_exponents[:, No...  219 us
    unnamed x2, local copies, waits for them, and re-layouts  9.27 us

profile of v3, /device:TPU:0, one launch (start us, length us, event | category | flops | bytes accessed | tf_op | source)
XLA Modules:
  0.0 229.4 jit_solution(6421605636509706311)
XLA Ops:
  0.6 219.5 %shard_map.194 = (bf16[4,8,512]{2,1,0:T(8,128)(2,1)}, f32[8,8,128,256]{3,2,1,0:T(8,128)}) custom-call(bf16[4,8,4096]{2,1,0:T(8,128)(2,1)} %hid_hbm.1, f32[1,4096]{1,0:T(1,128)} %bitcast.17, bf16[16,4096]{1,0:T(8,128)(2,1)} %bitcast.15, s32[8,2,8]{2,1,0:T(2,128)} %sc_hbm.1, s32[8,1,8]{2,1,0:T(1,128)} %bitcast.19, bf16[1024,1024]{1,0:T(8,128)(2,1)} %ocodes_hbm.1, ...), custom_call_target="tpu_custom_call" | custom-call | tf_op jit(solution)/shard_map/pallas_call | solution.py:470
  220.1 1.4 copy.24
  221.5 7.9 %copy.25 = f32[8,16,64,256]{3,2,1,0:T(8,128)} copy(f32[8,16,64,256]{3,2,1,0:T(8,128)} %bitcast.13) | data formatting | bytes 16777216

commit v4 on v3

--- a/solution.py
+++ b/solution.py
@@ -257,7 +257,7 @@
             if s == 0:
                 load.wait()
 
-            @pl.loop(0, nchunk)
+            @pl.loop(0, nchunk, unroll=2)
             def _(j):
                 full = jnp.concatenate(
                     [tbuf[j], jnp.zeros((LANES - 2 * rows, LANES), F32)], axis=0

time: 230 us -> 227 us (0.987)
    pallas_call x1, Pallas kernels: 219 us -> 217 us  [body(): call(hidden_in, pre_gain[None], w_dt.T, zx_exponents, out_exponents[:, No...]
where the time goes in v4:
time: 227 us
  Pallas kernels  217 us (96%)
  local copies, waits for them, and re-layouts  9.27 us (4%)
    pallas_call x1, Pallas kernels, body(): call(hidden_in, pre_gain[None], w_dt.T, zx_exponents, out_exponents[:, No...  217 us
    unnamed x2, local copies, waits for them, and re-layouts  9.27 us

profile of v4, /device:TPU:0, one launch (start us, length us, event | category | flops | bytes accessed | tf_op | source)
XLA Modules:
  0.0 226.8 jit_solution(3549390958798348422)
XLA Ops:
  0.6 216.9 %shard_map.194 = (bf16[4,8,512]{2,1,0:T(8,128)(2,1)}, f32[8,8,128,256]{3,2,1,0:T(8,128)}) custom-call(bf16[4,8,4096]{2,1,0:T(8,128)(2,1)} %hid_hbm.1, f32[1,4096]{1,0:T(1,128)} %bitcast.17, bf16[16,4096]{1,0:T(8,128)(2,1)} %bitcast.15, s32[8,2,8]{2,1,0:T(2,128)} %sc_hbm.1, s32[8,1,8]{2,1,0:T(1,128)} %bitcast.19, bf16[1024,1024]{1,0:T(8,128)(2,1)} %ocodes_hbm.1, ...), custom_call_target="tpu_custom_call" | custom-call | tf_op jit(solution)/shard_map/pallas_call | solution.py:470
  217.6 1.4 copy.24
  218.9 7.9 %copy.25 = f32[8,16,64,256]{3,2,1,0:T(8,128)} copy(f32[8,16,64,256]{3,2,1,0:T(8,128)} %bitcast.13) | data formatting | bytes 16777216
